TPU v7x, 32 devices: a whole 2x2x4 slice. The times are simulated.
32 devices in a mesh: groups: 2 (over x), mp: 16 (over z, y, core).
Axes of the slice: x: 2, y: 2, z: 4, core: 2. Of those that a mesh axis runs over, the one named last changes fastest.
Arguments:
- tokens: bfloat16 [512, 8192], P(('groups', 'mp')), parts along dimension 0, may hold values from -6 to 6
- queries: bfloat16 [512, 8192], P(('groups', 'mp')), parts along dimension 0, may hold values from -35 to 35
- key_proj: bfloat16 [512, 1024], P(('groups', 'mp')), parts along dimension 0, may hold values from -5 to 5
- values: bfloat16 [512, 1024], P(('groups', 'mp')), parts along dimension 0, may hold values from -6 to 6
- seq_lens: int32 [12], P('groups'), parts along dimension 0, may hold values from 21 to 85, as said below
- out_weight: bfloat16 [8192, 8192], P('mp'), may hold values from -0.25 to 0.25
- ffn_gain: float32 [2, 8192], replicated, may hold values from 0.25 to 2.5
- gate_weight: bfloat16 [8192, 12288], P(None, 'mp'), may hold values from -0.0625 to 0.0625
- up_weight: bfloat16 [8192, 12288], P(None, 'mp'), may hold values from -0.0625 to 0.0625
- down_weight: bfloat16 [12288, 8192], P('mp'), may hold values from -0.0546875 to 0.0546875
- slice_table: int32 [96], replicated, may hold values from 0 to 1, as said below
Outputs:
- stream: bfloat16 [512, 8192], P(('groups', 'mp')), parts along dimension 0
- mixed: bfloat16 [512, 8192], P(('groups', 'mp')), parts along dimension 0
There are 2 independent parts, one for each index of `groups`. A program takes and returns all parts, laid end to end along the dimension named above; an argument that names none is the same for every part. Nothing has to cross between parts.
Inputs may be any that keep to these rules, and one draw needn't show every extreme that they name: `seq_lens`: the 6 lengths sum to 256; the shortest is exactly 21 and the longest exactly 85. `slice_table`: exactly 16 entries are 1, the rest 0.
All inputs are finite; a program needn't handle non-finite values.
Results may differ from a plain program's by a relative error of at most 0.02.
Values may be sent and summed in bfloat16 or wider, within the bound.
A program may use at most 128 MiB of HBM per device.

v0:
```python
import math
import jax
import jax.numpy as jnp
from jax import lax
from jax.sharding import PartitionSpec as P

QUERY_HEADS = 64
HEAD_SIZE = 128
SLICE = 128


def segment_of(positions, seq_ends):
    return jnp.sum((positions[:, None] >= seq_ends[None, :]).astype(jnp.int32), axis=1)


def allowed(query_pos, key_pos, seq_ends):
    query_seg = segment_of(query_pos, seq_ends)
    key_seg = segment_of(key_pos, seq_ends)
    return (query_seg[:, None] == key_seg[None, :]) & (key_pos[None, :] <= query_pos[:, None])


def soft_weights(scores, visible):
    masked = jnp.where(visible, scores, -1e30)
    highest = jnp.max(masked, axis=-1, keepdims=True)
    expo = jnp.where(visible, jnp.exp(masked - highest), 0.0)
    return (expo / jnp.sum(expo, axis=-1, keepdims=True)).astype(jnp.bfloat16)


def rms_normed(stream_rows):
    stream_full = stream_rows.astype(jnp.float32)
    inv_rms = lax.rsqrt(jnp.mean(stream_full * stream_full, axis=1, keepdims=True) + 1e-05)
    return (stream_full * inv_rms).astype(jnp.bfloat16)


def local(
    tokens,
    queries,
    key_proj,
    values,
    seq_lens,
    out_weight,
    ffn_gain,
    gate_weight,
    up_weight,
    down_weight,
    slice_table,
):
    tok_dev = tokens.shape[0]
    my_index = lax.axis_index("mp")
    token_count = tok_dev * lax.axis_size("mp")
    heads_kv = key_proj.shape[1] // HEAD_SIZE
    query_heads_per_group = QUERY_HEADS // heads_kv
    score_scale = 1.0 / math.sqrt(HEAD_SIZE)
    key_all, value_all = (
        lax.all_gather(key_proj, "mp", axis=0, tiled=True),
        lax.all_gather(values, "mp", axis=0, tiled=True),
    )
    seq_ends = jnp.cumsum(seq_lens)
    key_pos = jnp.arange(token_count, dtype=jnp.int32)
    query_heads = lax.all_to_all(queries, "mp", split_axis=1, concat_axis=0, tiled=True)
    local_heads = query_heads.shape[1] // HEAD_SIZE
    kv_start = my_index * local_heads // query_heads_per_group * HEAD_SIZE
    key_cols = lax.dynamic_slice_in_dim(key_all, kv_start, HEAD_SIZE, 1)
    value_cols = lax.dynamic_slice_in_dim(value_all, kv_start, HEAD_SIZE, 1)
    visible = allowed(key_pos, key_pos, seq_ends)
    scores = (
        jnp.einsum(
            "thd,sd->hts",
            query_heads.reshape(token_count, local_heads, HEAD_SIZE),
            key_cols,
            preferred_element_type=jnp.float32,
        )
        * score_scale
    )
    attn_probs = soft_weights(scores, visible[None])
    context = (
        jnp.einsum("hts,sd->thd", attn_probs, value_cols, preferred_element_type=jnp.float32)
        .astype(jnp.bfloat16)
        .reshape(token_count, local_heads * HEAD_SIZE)
    )
    picked = context
    attn_share = lax.psum_scatter(
        jnp.dot(picked, out_weight, preferred_element_type=jnp.float32).astype(jnp.bfloat16),
        "mp",
        scatter_dimension=0,
        tiled=True,
    ).astype(jnp.float32)
    stream = (tokens.astype(jnp.float32) + attn_share).astype(jnp.bfloat16)
    sent_rows = rms_normed(stream)
    slice_count = gate_weight.shape[1] // SLICE
    row_piece = lax.all_gather(sent_rows, "mp", axis=0, tiled=True)
    outputs = []
    for slice_pos in range(slice_count):
        ffn_which = lax.dynamic_index_in_dim(
            slice_table, my_index * slice_count + slice_pos, 0, keepdims=False
        )
        gain_row = lax.dynamic_index_in_dim(ffn_gain, ffn_which, 0, keepdims=False)
        slice_input = (row_piece.astype(jnp.float32) * gain_row[None, :]).astype(jnp.bfloat16)
        gate_val = jnp.dot(
            slice_input,
            gate_weight[:, slice_pos * SLICE : (slice_pos + 1) * SLICE],
            preferred_element_type=jnp.float32,
        )
        up_val = jnp.dot(
            slice_input,
            up_weight[:, slice_pos * SLICE : (slice_pos + 1) * SLICE],
            preferred_element_type=jnp.float32,
        )
        outputs.append((jax.nn.silu(gate_val) * up_val).astype(jnp.bfloat16))
    hidden = jnp.concatenate(outputs, axis=1)
    picked = hidden
    ffn_share = lax.psum_scatter(
        jnp.dot(picked, down_weight, preferred_element_type=jnp.float32).astype(jnp.bfloat16),
        "mp",
        scatter_dimension=0,
        tiled=True,
    ).astype(jnp.float32)
    mixed = (stream.astype(jnp.float32) + ffn_share).astype(jnp.bfloat16)
    return (stream, mixed)


def solution(mesh):
    placed = (
        P(("groups", "mp"), None),
        P(("groups", "mp"), None),
        P(("groups", "mp"), None),
        P(("groups", "mp"), None),
        P("groups"),
        P("mp", None),
        P(),
        P(None, "mp"),
        P(None, "mp"),
        P("mp", None),
        P(),
    )
    return jax.shard_map(
        local,
        mesh=mesh,
        in_specs=placed,
        out_specs=(P(("groups", "mp"), None), P(("groups", "mp"), None)),
        check_vma=False,
    )
```

profile of v0, /device:TPU:0, one launch (start us, length us, event | category | flops | bytes accessed | tf_op | source)
XLA Modules:
  0.0 304.8 jit_solution(16253626223594990531)
XLA Ops:
  7.2 1.7 copy.43
  8.8 7.4 %all-to-all-start = ((bf16[16,16,512]{2,0,1:T(8,128)(2,1)}), bf16[16,16,512]{2,0,1:T(8,128)(2,1)S(1)}, u32[]{:S(2)}, u32[]{:S(2)}) async-start(bf16[16,16,512]{2,0,1:T(8,128)(2,1)} %bitcast.57), calls=%async_computation | async-start | bytes 524288 | tf_op jit(solution)/shard_map/all_to_all | solution.py:60
  16.2 0.0 reduce-scatter.3.cloned.1.call-start
  16.3 0.8 reduce-window.8
  17.1 0.1 convert_reduce_fusion
  17.2 0.1 fusion.142
  17.3 23.5 %all_gather.10 = bf16[256,1024]{1,0:T(8,128)(2,1)S(1)} all-gather(bf16[16,1024]{1,0:T(8,128)(2,1)} %param.13), channel_id=1, replica_groups=mesh['groups'=2,'mp'=16] {'mp'}, dimensions={0}, use_global_device_ids=true | all-gather | bytes 557056 | tf_op jit(solution)/shard_map/all_gather | solution.py:55
  40.8 19.1 %all_gather.9 = bf16[256,1024]{1,0:T(8,128)(2,1)S(1)} all-gather(bf16[16,1024]{1,0:T(8,128)(2,1)} %param.14), channel_id=1, replica_groups=mesh['groups'=2,'mp'=16] {'mp'}, dimensions={0}, use_global_device_ids=true | all-gather | bytes 557056 | tf_op jit(solution)/shard_map/all_gather | solution.py:56
  59.9 0.0 all-to-all-done
  59.9 0.1 reshape.90
  60.0 0.6 fusion.181
  60.6 0.8 convolution_convert_fusion.2
  61.4 7.7 %convolution_convert_fusion = bf16[256,8192]{1,0:T(8,128)(2,1)} fusion(bf16[256,512]{0,1:T(8,128)(2,1)S(1)} %bitcast.61, bf16[512,8192]{1,0:T(8,128)(2,1)} %param.16), kind=kOutput, calls=%fused_computation.7 | convolution fusion | flops 2149580800 | bytes 12845056 | tf_op jit(solution)/shard_map/dot_general | solution.py:83
  69.1 0.0 copy-start.2
  69.1 0.0 copy-start.3
  69.1 0.0 reduce-scatter.3.cloned.1.call-update
  69.1 0.0 all-gather.2.cloned.1.call-start
  69.2 70.8 %reduce-scatter.3.cloned.1.call-done = bf16[16,8192]{1,0:T(8,128)(2,1)} async-done(((bf16[256,8192]{1,0:T(8,128)(2,1)}), bf16[16,8192]{1,0:T(8,128)(2,1)}) %reduce-scatter.3.cloned.1.call-update) | async-done | bytes 262160 | tf_op jit(solution)/shard_map/reduce_scatter | solution.py:82
  140.0 0.0 copy-done.2
  140.0 1.2 fusion.138
  141.2 0.8 fusion.139
  142.0 0.0 all-gather.2.cloned.1.call-update
  142.1 0.2 reduce-scatter.5.cloned.1.call-start
  142.3 0.0 copy-done.3
  142.3 0.7 fusion.180
  154.1 0.0 copy-done.1
  154.1 0.2 constant_dynamic-slice_fusion
  154.3 38.4 %all-gather.2.cloned.1.call-done = bf16[256,8192]{1,0:T(8,128)(2,1)} async-done(((bf16[16,8192]{1,0:T(8,128)(2,1)}), bf16[256,8192]{1,0:T(8,128)(2,1)}) %all-gather.2.cloned.1.call-update) | async-done | bytes 4194320 | tf_op jit(solution)/shard_map/all_gather | solution.py:91
  192.6 4.4 %fusion.29 = f32[256,128]{0,1:T(8,128)S(1)} fusion(bf16[256,8192]{1,0:T(8,128)(2,1)} %all-gather.2.cloned.1.call-done, f32[8192]{0:T(1024)S(1)} %bitcast.73, bf16[8192,768]{1,0:T(8,128)(2,1)} %param.18), kind=kOutput, calls=%fused_computation.26 | convolution fusion | flops 543162368 | bytes 6455296 | tf_op jit(solution)/shard_map/dot_general | solution.py:99
  197.1 0.0 copy-done.4
  197.1 0.0 slice-start.4
  197.1 3.2 %fusion.25 = f32[256,128]{0,1:T(8,128)S(1)} fusion(bf16[256,8192]{1,0:T(8,128)(2,1)S(1)} %copy-done.4, f32[8192]{0:T(1024)S(1)} %bitcast.71, bf16[8192,768]{1,0:T(8,128)(2,1)} %param.18), kind=kOutput, calls=%fused_computation.24 | convolution fusion | flops 543162368 | bytes 6455296 | tf_op jit(solution)/shard_map/dot_general | solution.py:99
  200.3 0.0 slice-start.5
  200.3 3.2 %fusion.21 = f32[256,128]{0,1:T(8,128)S(1)} fusion(bf16[256,8192]{1,0:T(8,128)(2,1)S(1)} %copy-done.4, f32[8192]{0:T(1024)S(1)} %bitcast.69, bf16[8192,768]{1,0:T(8,128)(2,1)} %param.18), kind=kOutput, calls=%fused_computation.22 | convolution fusion | flops 543162368 | bytes 6455296 | tf_op jit(solution)/shard_map/dot_general | solution.py:99
  203.5 0.0 slice-done.3
  203.5 0.0 slice-done.4
  203.5 0.0 slice-done.5
  203.5 0.0 slice-start.6
  203.5 1.5 fusion.17
  205.0 0.0 slice-start.7
  205.1 1.5 fusion.13
  206.5 0.0 slice-start.8
  206.6 1.5 fusion.9
  208.1 0.0 slice-done.6
  208.1 0.0 slice-done.7
  208.1 0.9 slice-done.8
  209.0 1.4 fusion.108
  210.4 1.4 fusion.113
  211.8 1.5 fusion.118
  213.3 0.0 copy-start.5
  213.3 0.0 slice-start
  213.3 1.6 fusion.123
  214.9 0.5 copy-done.5
  215.5 1.5 fusion.128
  216.9 0.0 slice-start.2
  216.9 3.2 %fusion.133 = bf16[256,768]{0,1:T(8,128)(2,1)S(1)} fusion(bf16[256,768]{0,1:T(8,128)(2,1)S(1)} %fusion.128, bf16[8192,768]{1,0:T(8,128)(2,1)} %param.19, bf16[256,8192]{1,0:T(8,128)(2,1)S(1)} %copy-done.5, f32[8192]{0:T(1024)S(1)} %bitcast.64, f32[256,128]{0,1:T(8,128)S(1)} %fusion.9), kind=kOutput, calls=%fused_computation.63 | convolution fusion | flops 543358976 | bytes 6520832 | tf_op jit(solution)/shard_map/dot_general | solution.py:104
  220.2 0.0 slice-done
  220.2 0.0 slice-done.1
  220.2 0.0 slice-done.2
  220.2 5.1 %convolution_convert_fusion.1 = bf16[256,8192]{1,0:T(8,128)(2,1)} fusion(bf16[256,768]{0,1:T(8,128)(2,1)S(1)} %fusion.133, bf16[768,8192]{1,0:T(8,128)(2,1)S(1)} %bitcast.59), kind=kOutput, calls=%fused_computation.8 | convolution fusion | flops 3223322624 | bytes 17170432 | tf_op jit(solution)/shard_map/dot_general | solution.py:113
  225.3 0.0 reduce-scatter.5.cloned.1.call-update
  225.3 71.3 %reduce-scatter.5.cloned.1.call-done = bf16[16,8192]{1,0:T(8,128)(2,1)} async-done(((bf16[256,8192]{1,0:T(8,128)(2,1)}), bf16[16,8192]{1,0:T(8,128)(2,1)}) %reduce-scatter.5.cloned.1.call-update) | async-done | bytes 262160 | tf_op jit(solution)/shard_map/reduce_scatter | solution.py:112
  296.6 0.0 copy-done
  296.6 1.7 fusion.140
  (9 shorter events, 0.0 us)
Async XLA Ops:
  8.8 51.1 %all-to-all-start = ((bf16[16,16,512]{2,0,1:T(8,128)(2,1)}), bf16[16,16,512]{2,0,1:T(8,128)(2,1)S(1)}, u32[]{:S(2)}, u32[]{:S(2)}) async-start(bf16[16,16,512]{2,0,1:T(8,128)(2,1)} %bitcast.57), calls=%async_computation | async-start | bytes 524288 | tf_op jit(solution)/shard_map/all_to_all | solution.py:60
  16.2 123.8 %reduce-scatter.3.cloned.1.call-start = ((), (), s32[]{:S(2)}) async-start(), calls=%async_computation.3 | async-start | bytes 4456448 | tf_op jit(solution)/shard_map/reduce_scatter | solution.py:82
  69.1 70.9 %copy-start.2 = (bf16[16,8192]{1,0:T(8,128)(2,1)S(1)}, bf16[16,8192]{1,0:T(8,128)(2,1)}, u32[]{:S(2)}) copy-start(bf16[16,8192]{1,0:T(8,128)(2,1)} %param.11) | copy-start | bytes 786436
  69.1 73.2 %copy-start.3 = (s32[96]{0:T(128)S(1)}, s32[96]{0:T(128)}, u32[]{:S(2)}) copy-start(s32[96]{0:T(128)} %param.21) | copy-start | bytes 1156
  69.1 85.0 %copy-start.1 = (f32[2,8192]{1,0:T(2,128)S(1)}, f32[2,8192]{1,0:T(2,128)}, u32[]{:S(2)}) copy-start(f32[2,8192]{1,0:T(2,128)} %param.17) | copy-start | bytes 196612
  69.1 123.5 %all-gather.2.cloned.1.call-start = ((), (), s32[]{:S(2)}) async-start(), calls=%async_computation.4 | async-start | bytes 4456448 | tf_op jit(solution)/shard_map/all_gather | solution.py:91
  141.2 155.4 %copy-start = (bf16[16,8192]{1,0:T(8,128)(2,1)}, bf16[16,8192]{1,0:T(8,128)(2,1)S(1)}, u32[]{:S(2)}) copy-start(bf16[16,8192]{1,0:T(8,128)(2,1)S(1)} %get-tuple-element.3) | copy-start | bytes 786436
  142.1 154.5 %reduce-scatter.5.cloned.1.call-start = ((), (), s32[]{:S(2)}) async-start(), calls=%async_computation.5 | async-start | bytes 4456448 | tf_op jit(solution)/shard_map/reduce_scatter | solution.py:112
  192.6 4.5 %copy-start.4 = (bf16[256,8192]{1,0:T(8,128)(2,1)S(1)}, bf16[256,8192]{1,0:T(8,128)(2,1)}, u32[]{:S(2)}) copy-start(bf16[256,8192]{1,0:T(8,128)(2,1)} %all-gather.2.cloned.1.call-done) | copy-start | bytes 12582916
  192.6 10.8 %slice-start.3 = ((s8[12582912]{0:T(1024)(128)(4,1)}), s8[4194304]{0:T(1024)(128)(4,1)S(1)}, s32[]{:S(2)}) async-start(s8[12582912]{0:T(1024)(128)(4,1)} %bitcast.75), calls=%async_computation.9 | async-start | bytes 8388608
  197.1 6.4 %slice-start.4 = ((s8[12582912]{0:T(1024)(128)(4,1)}), s8[4194304]{0:T(1024)(128)(4,1)S(1)}, s32[]{:S(2)}) async-start(s8[12582912]{0:T(1024)(128)(4,1)} %bitcast.75), calls=%async_computation.10 | async-start | bytes 8388608
  200.3 3.2 %slice-start.5 = ((s8[12582912]{0:T(1024)(128)(4,1)}), s8[4194304]{0:T(1024)(128)(4,1)S(1)}, s32[]{:S(2)}) async-start(s8[12582912]{0:T(1024)(128)(4,1)} %bitcast.75), calls=%async_computation.11 | async-start | bytes 8388608
  203.5 4.6 %slice-start.6 = ((s8[12582912]{0:T(1024)(128)(4,1)}), s8[4194304]{0:T(1024)(128)(4,1)S(1)}, s32[]{:S(2)}) async-start(s8[12582912]{0:T(1024)(128)(4,1)} %bitcast.77), calls=%async_computation.12 | async-start | bytes 8388608
  205.0 3.0 slice-start.7
  206.5 2.4 slice-start.8
  213.3 2.2 copy-start.5
  213.3 6.9 %slice-start = ((s8[12582912]{0:T(1024)(128)(4,1)}), s8[4194304]{0:T(1024)(128)(4,1)S(1)}, s32[]{:S(2)}) async-start(s8[12582912]{0:T(1024)(128)(4,1)} %bitcast.58), calls=%async_computation.6 | async-start | bytes 8388608
  215.5 4.7 %slice-start.1 = ((s8[12582912]{0:T(1024)(128)(4,1)}), s8[4194304]{0:T(1024)(128)(4,1)S(1)}, s32[]{:S(2)}) async-start(s8[12582912]{0:T(1024)(128)(4,1)} %bitcast.58), calls=%async_computation.7 | async-start | bytes 8388608
  216.9 3.3 %slice-start.2 = ((s8[12582912]{0:T(1024)(128)(4,1)}), s8[4194304]{0:T(1024)(128)(4,1)S(1)}, s32[]{:S(2)}) async-start(s8[12582912]{0:T(1024)(128)(4,1)} %bitcast.58), calls=%async_computation.8 | async-start | bytes 8388608
Sparse Core Ops, SparseCore 0:
  69.2 70.7 reduce-scatter.2
  143.0 49.6 all-gather.1
  225.4 71.1 reduce-scatter.4
where the time goes:
time: 305 us
  waiting for transfers between devices  181 us (59%)
  blocking collectives  42.6 us (14%)
  matrix products  40 us (13%)
  between operations  25.2 us (8%)
  starting transfers between devices  7.69 us (3%)
  other arithmetic  4.74 us (2%)
  local copies, waits for them, and re-layouts  4.1 us (1%)
    reduce_scatter x1, waiting for transfers between devices, local(): lax.psum_scatter(jnp.dot(picked, down_weight, preferred_element_type=jnp....  71.3 us
    reduce_scatter x1, waiting for transfers between devices, local(): lax.psum_scatter(jnp.dot(picked, out_weight, preferred_element_type=jnp.f...  70.8 us
    all_gather x1, waiting for transfers between devices, local(): row_piece = lax.all_gather(sent_rows, 'mp', axis=0, tiled=True)  38.4 us
    all_gather x1, blocking collectives, local(): lax.all_gather(key_proj, 'mp', axis=0, tiled=True)  23.5 us
    all_gather x1, blocking collectives, local(): lax.all_gather(values, 'mp', axis=0, tiled=True)  19.1 us
    dot_general x6, matrix products, local(): jnp.dot(slice_input, gate_weight[:, slice_pos * SLICE:(slice_pos + 1) * S...  15.3 us
    dot_general x6, matrix products, local(): jnp.dot(slice_input, up_weight[:, slice_pos * SLICE:(slice_pos + 1) * SLI...  10.6 us
    dot_general x1, matrix products, local(): jnp.dot(picked, out_weight, preferred_element_type=jnp.float32)  7.71 us
  transfers between devices with their start and end apart: 4, of which 3 were waited for; matrix products, arithmetic and copies ran while one was open for 1% of the time, Pallas kernels for 0%

commit v1 on v0

--- a/solution.py
+++ b/solution.py
@@ -57,7 +57,17 @@
     )
     seq_ends = jnp.cumsum(seq_lens)
     key_pos = jnp.arange(token_count, dtype=jnp.int32)
-    query_heads = lax.all_to_all(queries, "mp", split_axis=1, concat_axis=0, tiled=True)
+
+    def replace_classes(point, axis_key):
+        carry_out = jnp.concatenate(
+            lax.all_to_all(
+                jnp.stack(jnp.split(point, lax.axis_size(axis_key), axis=1), 0), axis_key, 0, 0
+            ),
+            0,
+        )
+        return carry_out
+
+    query_heads = replace_classes(queries, "mp")
     local_heads = query_heads.shape[1] // HEAD_SIZE
     kv_start = my_index * local_heads // query_heads_per_group * HEAD_SIZE
     key_cols = lax.dynamic_slice_in_dim(key_all, kv_start, HEAD_SIZE, 1)

time: 305 us -> 326 us (1.069)
  local copies, waits for them, and re-layouts: 4.1 us -> 23.6 us
    unnamed x30 -> x45, local copies, waits for them, and re-layouts: 1.48 us -> 21.3 us
where the time goes in v1:
time: 326 us; the launch traced here: 324 us
  waiting for transfers between devices  180 us (55%)
  blocking collectives  42.6 us (13%)
  matrix products  40 us (12%)
  between operations  25.2 us (8%)
  local copies, waits for them, and re-layouts  23.6 us (7%)
  starting transfers between devices  7.69 us (2%)
  other arithmetic  4.74 us (1%)
    reduce_scatter x1, waiting for transfers between devices, local(): lax.psum_scatter(jnp.dot(picked, down_weight, preferred_element_type=jnp....  71.1 us
    reduce_scatter x1, waiting for transfers between devices, local(): lax.psum_scatter(jnp.dot(picked, out_weight, preferred_element_type=jnp.f...  71 us
    all_gather x1, waiting for transfers between devices, local(): row_piece = lax.all_gather(sent_rows, 'mp', axis=0, tiled=True)  38.3 us
    all_gather x1, blocking collectives, local(): lax.all_gather(key_proj, 'mp', axis=0, tiled=True)  23.5 us
    unnamed x45, local copies, waits for them, and re-layouts  21.3 us
    all_gather x1, blocking collectives, local(): lax.all_gather(values, 'mp', axis=0, tiled=True)  19.1 us
    dot_general x6, matrix products, local(): jnp.dot(slice_input, gate_weight[:, slice_pos * SLICE:(slice_pos + 1) * S...  15.3 us
    dot_general x6, matrix products, local(): jnp.dot(slice_input, up_weight[:, slice_pos * SLICE:(slice_pos + 1) * SLI...  10.6 us
  transfers between devices with their start and end apart: 4, of which 3 were waited for; matrix products, arithmetic and copies ran while one was open for 1% of the time, Pallas kernels for 0%

profile of v1, /device:TPU:0, one launch (start us, length us, event | category | flops | bytes accessed | tf_op | source)
XLA Modules:
  0.0 324.1 jit_solution(379861838894190509)
XLA Ops:
  7.2 1.3 constant_dynamic-update-slice_fusion.15
  8.5 1.3 constant_dynamic-update-slice_fusion.14
  9.8 1.3 constant_dynamic-update-slice_fusion.13
  11.1 1.3 constant_dynamic-update-slice_fusion.12
  12.5 1.3 constant_dynamic-update-slice_fusion.11
  13.8 1.3 constant_dynamic-update-slice_fusion.10
  15.1 1.3 constant_dynamic-update-slice_fusion.9
  16.4 1.3 constant_dynamic-update-slice_fusion.8
  17.8 1.3 constant_dynamic-update-slice_fusion.7
  19.1 1.3 constant_dynamic-update-slice_fusion.6
  20.4 1.3 constant_dynamic-update-slice_fusion.5
  21.7 1.3 constant_dynamic-update-slice_fusion.4
  23.0 1.3 constant_dynamic-update-slice_fusion.3
  24.4 1.3 constant_dynamic-update-slice_fusion.2
  25.7 1.3 constant_dynamic-update-slice_fusion.1
  27.0 1.3 constant_dynamic-update-slice_fusion
  28.3 7.4 %all-to-all-start = ((bf16[16,16,512]{2,1,0:T(8,128)(2,1)}), bf16[16,16,512]{2,1,0:T(8,128)(2,1)S(1)}, u32[]{:S(2)}, u32[]{:S(2)}) async-start(bf16[16,16,512]{2,1,0:T(8,128)(2,1)} %constant_dynamic-update-slice_fusion), calls=%async_computation | async-start | bytes 524288 | tf_op jit(solution)/shard_map/all_to_all | solution.py:63
  35.7 0.0 reduce-scatter.3.cloned.1.call-start
  35.8 0.8 reduce-window.8
  36.6 0.1 convert_reduce_fusion
  36.7 0.1 fusion.142
  36.8 23.5 %all_gather.10 = bf16[256,1024]{1,0:T(8,128)(2,1)S(1)} all-gather(bf16[16,1024]{1,0:T(8,128)(2,1)} %param.13), channel_id=1, replica_groups=mesh['groups'=2,'mp'=16] {'mp'}, dimensions={0}, use_global_device_ids=true | all-gather | bytes 557056 | tf_op jit(solution)/shard_map/all_gather | solution.py:55
  60.3 19.1 %all_gather.9 = bf16[256,1024]{1,0:T(8,128)(2,1)S(1)} all-gather(bf16[16,1024]{1,0:T(8,128)(2,1)} %param.14), channel_id=1, replica_groups=mesh['groups'=2,'mp'=16] {'mp'}, dimensions={0}, use_global_device_ids=true | all-gather | bytes 557056 | tf_op jit(solution)/shard_map/all_gather | solution.py:56
  79.4 0.0 all-to-all-done
  79.4 0.1 reshape_reshape.3
  79.5 0.6 fusion.181
  80.1 0.8 convolution_convert_fusion.2
  80.9 7.7 %convolution_convert_fusion = bf16[256,8192]{1,0:T(8,128)(2,1)} fusion(bf16[256,512]{0,1:T(8,128)(2,1)S(1)} %bitcast.87, bf16[512,8192]{1,0:T(8,128)(2,1)} %param.16), kind=kOutput, calls=%fused_computation.7 | convolution fusion | flops 2149580800 | bytes 12845056 | tf_op jit(solution)/shard_map/dot_general | solution.py:93
  88.6 0.0 reduce-scatter.3.cloned.1.call-update
  88.6 0.0 all-gather.2.cloned.1.call-start
  88.7 71.0 %reduce-scatter.3.cloned.1.call-done = bf16[16,8192]{1,0:T(8,128)(2,1)} async-done(((bf16[256,8192]{1,0:T(8,128)(2,1)}), bf16[16,8192]{1,0:T(8,128)(2,1)}) %reduce-scatter.3.cloned.1.call-update) | async-done | bytes 262160 | tf_op jit(solution)/shard_map/reduce_scatter | solution.py:92
  159.6 1.2 fusion.138
  160.8 0.8 fusion.139
  161.6 0.0 all-gather.2.cloned.1.call-update
  161.7 0.2 reduce-scatter.5.cloned.1.call-start
  161.9 0.0 copy-done.3
  161.9 0.7 fusion.180
  173.7 0.2 constant_dynamic-slice_fusion
  173.9 38.3 %all-gather.2.cloned.1.call-done = bf16[256,8192]{1,0:T(8,128)(2,1)} async-done(((bf16[16,8192]{1,0:T(8,128)(2,1)}), bf16[256,8192]{1,0:T(8,128)(2,1)}) %all-gather.2.cloned.1.call-update) | async-done | bytes 4194320 | tf_op jit(solution)/shard_map/all_gather | solution.py:101
  212.2 4.4 %fusion.29 = f32[256,128]{0,1:T(8,128)S(1)} fusion(bf16[256,8192]{1,0:T(8,128)(2,1)} %all-gather.2.cloned.1.call-done, f32[8192]{0:T(1024)S(1)} %bitcast.98, bf16[8192,768]{1,0:T(8,128)(2,1)} %param.18), kind=kOutput, calls=%fused_computation.26 | convolution fusion | flops 543162368 | bytes 6455296 | tf_op jit(solution)/shard_map/dot_general | solution.py:109
  216.6 0.0 slice-start.4
  216.6 3.2 fusion.25
  219.8 0.0 slice-start.5
  219.8 3.2 fusion.21
  223.0 0.0 slice-start.6
  223.0 1.5 fusion.17
  224.6 0.0 slice-start.7
  224.6 1.5 fusion.13
  226.1 0.0 slice-start.8
  226.1 1.5 fusion.9
  227.6 0.9 slice-done.8
  228.5 1.4 fusion.108
  229.9 1.4 fusion.113
  231.3 1.5 fusion.118
  232.8 0.0 slice-start
  232.8 1.6 fusion.123
  234.4 0.5 copy-done.5
  235.0 1.5 fusion.128
  236.4 0.0 slice-start.2
  236.5 3.2 fusion.133
  239.7 5.1 %convolution_convert_fusion.1 = bf16[256,8192]{1,0:T(8,128)(2,1)} fusion(bf16[256,768]{0,1:T(8,128)(2,1)S(1)} %fusion.133, bf16[768,8192]{1,0:T(8,128)(2,1)S(1)} %bitcast.86), kind=kOutput, calls=%fused_computation.8 | convolution fusion | flops 3223322624 | bytes 17170432 | tf_op jit(solution)/shard_map/dot_general | solution.py:123
  244.8 0.0 reduce-scatter.5.cloned.1.call-update
  244.8 71.1 %reduce-scatter.5.cloned.1.call-done = bf16[16,8192]{1,0:T(8,128)(2,1)} async-done(((bf16[256,8192]{1,0:T(8,128)(2,1)}), bf16[16,8192]{1,0:T(8,128)(2,1)}) %reduce-scatter.5.cloned.1.call-update) | async-done | bytes 262160 | tf_op jit(solution)/shard_map/reduce_scatter | solution.py:122
  315.9 1.7 fusion.140
  (24 shorter events, 0.0 us)
Async XLA Ops:
  28.3 51.1 %all-to-all-start = ((bf16[16,16,512]{2,1,0:T(8,128)(2,1)}), bf16[16,16,512]{2,1,0:T(8,128)(2,1)S(1)}, u32[]{:S(2)}, u32[]{:S(2)}) async-start(bf16[16,16,512]{2,1,0:T(8,128)(2,1)} %constant_dynamic-update-slice_fusion), calls=%async_computation | async-start | bytes 524288 | tf_op jit(solution)/shard_map/all_to_all | solution.py:63
  35.7 123.9 %reduce-scatter.3.cloned.1.call-start = ((), (), s32[]{:S(2)}) async-start(), calls=%async_computation.3 | async-start | bytes 4456448 | tf_op jit(solution)/shard_map/reduce_scatter | solution.py:92
  88.6 71.0 %copy-start.2 = (bf16[16,8192]{1,0:T(8,128)(2,1)S(1)}, bf16[16,8192]{1,0:T(8,128)(2,1)}, u32[]{:S(2)}) copy-start(bf16[16,8192]{1,0:T(8,128)(2,1)} %param.11) | copy-start | bytes 786436
  88.6 73.3 %copy-start.3 = (s32[96]{0:T(128)S(1)}, s32[96]{0:T(128)}, u32[]{:S(2)}) copy-start(s32[96]{0:T(128)} %param.21) | copy-start | bytes 1156
  88.6 85.1 %copy-start.1 = (f32[2,8192]{1,0:T(2,128)S(1)}, f32[2,8192]{1,0:T(2,128)}, u32[]{:S(2)}) copy-start(f32[2,8192]{1,0:T(2,128)} %param.17) | copy-start | bytes 196612
  88.6 123.6 %all-gather.2.cloned.1.call-start = ((), (), s32[]{:S(2)}) async-start(), calls=%async_computation.4 | async-start | bytes 4456448 | tf_op jit(solution)/shard_map/all_gather | solution.py:101
  160.8 155.1 %copy-start = (bf16[16,8192]{1,0:T(8,128)(2,1)}, bf16[16,8192]{1,0:T(8,128)(2,1)S(1)}, u32[]{:S(2)}) copy-start(bf16[16,8192]{1,0:T(8,128)(2,1)S(1)} %get-tuple-element.3) | copy-start | bytes 786436
  161.7 154.2 %reduce-scatter.5.cloned.1.call-start = ((), (), s32[]{:S(2)}) async-start(), calls=%async_computation.5 | async-start | bytes 4456448 | tf_op jit(solution)/shard_map/reduce_scatter | solution.py:122
  212.2 4.4 %copy-start.4 = (bf16[256,8192]{1,0:T(8,128)(2,1)S(1)}, bf16[256,8192]{1,0:T(8,128)(2,1)}, u32[]{:S(2)}) copy-start(bf16[256,8192]{1,0:T(8,128)(2,1)} %all-gather.2.cloned.1.call-done) | copy-start | bytes 12582916
  212.2 10.8 %slice-start.3 = ((s8[12582912]{0:T(1024)(128)(4,1)}), s8[4194304]{0:T(1024)(128)(4,1)S(1)}, s32[]{:S(2)}) async-start(s8[12582912]{0:T(1024)(128)(4,1)} %bitcast.100), calls=%async_computation.9 | async-start | bytes 8388608
  216.6 6.4 %slice-start.4 = ((s8[12582912]{0:T(1024)(128)(4,1)}), s8[4194304]{0:T(1024)(128)(4,1)S(1)}, s32[]{:S(2)}) async-start(s8[12582912]{0:T(1024)(128)(4,1)} %bitcast.100), calls=%async_computation.10 | async-start | bytes 8388608
  219.8 3.2 slice-start.5
  223.0 4.6 %slice-start.6 = ((s8[12582912]{0:T(1024)(128)(4,1)}), s8[4194304]{0:T(1024)(128)(4,1)S(1)}, s32[]{:S(2)}) async-start(s8[12582912]{0:T(1024)(128)(4,1)} %bitcast.102), calls=%async_computation.12 | async-start | bytes 8388608
  224.6 3.0 slice-start.7
  226.1 2.4 slice-start.8
  232.8 2.2 copy-start.5
  232.8 6.9 %slice-start = ((s8[12582912]{0:T(1024)(128)(4,1)}), s8[4194304]{0:T(1024)(128)(4,1)S(1)}, s32[]{:S(2)}) async-start(s8[12582912]{0:T(1024)(128)(4,1)} %bitcast.85), calls=%async_computation.6 | async-start | bytes 8388608
  235.0 4.7 %slice-start.1 = ((s8[12582912]{0:T(1024)(128)(4,1)}), s8[4194304]{0:T(1024)(128)(4,1)S(1)}, s32[]{:S(2)}) async-start(s8[12582912]{0:T(1024)(128)(4,1)} %bitcast.85), calls=%async_computation.7 | async-start | bytes 8388608
  236.4 3.3 %slice-start.2 = ((s8[12582912]{0:T(1024)(128)(4,1)}), s8[4194304]{0:T(1024)(128)(4,1)S(1)}, s32[]{:S(2)}) async-start(s8[12582912]{0:T(1024)(128)(4,1)} %bitcast.85), calls=%async_computation.8 | async-start | bytes 8388608
Sparse Core Ops, SparseCore 0:
  88.7 70.8 reduce-scatter.2
  162.6 49.5 all-gather.1
  245.0 70.8 reduce-scatter.4
